TPU v7x, 32 devices: a whole 2x2x4 slice. The times are simulated.
32 devices in a mesh: grp: 4 (over z), tile: 8 (over y, x, core).
Axes of the slice: x: 2, y: 2, z: 4, core: 2. Of those that a mesh axis runs over, the one named last changes fastest.
Arguments:
- right_side: float32 [16, 32768], P(None, ('grp', 'tile')), may hold values from -6 to 6
- ridge: float32 [32768], P(('grp', 'tile')), may hold values from 1 to 4
- tiles: float32 [128, 1024, 1024], P(('grp', 'tile')), may hold values from -0.013671875 to 0.013671875
- tile_list: int32 [128, 2], P(('grp', 'tile')), may hold values from 0 to 31, as said below
Outputs:
- solution: float32 [16, 32768], P(None, ('grp', 'tile'))
- residual: float32 [16, 32768], P(None, ('grp', 'tile'))
Inputs may be any that keep to these rules, and one draw needn't show every extreme that they name: `tile_list`: each row is a pair (row block, column block) with row block >= column block; no pair appears twice; rows stand in packed row-major order (row block rising, then column block rising).
All inputs are finite; a program needn't handle non-finite values.
Results may differ from a plain program's by a relative error of at most 0.0003.
Values sent between devices are 32-bit elements; how exact they have to be, the bound alone decides.
A program may use at most 64 MiB of HBM per device.

v0:
```python
import jax
import jax.numpy as jnp
from jax import lax
from jax.sharding import PartitionSpec as P

ITERS = 2


def gauss_solve(matrix, rhs):
    order = matrix.shape[0]
    for pivot in range(order):
        scale = 1.0 / matrix[pivot, pivot]
        row_new = matrix[pivot] * scale
        rhs_new = rhs[pivot] * scale
        factor = matrix[:, pivot] * (1.0 - (jnp.arange(order) == pivot).astype(matrix.dtype))
        matrix = matrix - factor[:, None] * row_new[None, :]
        rhs = rhs - factor[:, None] * rhs_new[None, :]
        matrix = matrix.at[pivot].set(row_new)
        rhs = rhs.at[pivot].set(rhs_new)
    return rhs


def gram(left, right):
    return lax.dot_general(
        left,
        right,
        (((1,), (1,)), ((), ())),
        precision=lax.Precision.HIGHEST,
        preferred_element_type=jnp.float32,
    )


def mixed(coeffs, rows):
    return jnp.dot(coeffs.T, rows, precision=lax.Precision.HIGHEST)


def tile_masks(order):
    rowid = lax.broadcasted_iota(jnp.int32, (order, order), 0)
    colid = lax.broadcasted_iota(jnp.int32, (order, order), 1)
    return (rowid >= colid, rowid > colid)


def apply_kernel(tiles, tile_list, field):
    order = tiles.shape[1]
    lower, strict = tile_masks(order)

    def step(total, item):
        tile, pair = item
        block_row = pair[0]
        block_col = pair[1]
        differ = block_row != block_col
        direct_tile = jnp.where(jnp.logical_or(lower, differ), tile, jnp.zeros_like(tile))
        mirror_tile = jnp.where(jnp.logical_or(strict, differ), tile, jnp.zeros_like(tile))
        row_start = block_row * order
        col_start = block_col * order
        from_col = lax.dynamic_slice_in_dim(field, col_start, order, 1)
        from_row = lax.dynamic_slice_in_dim(field, row_start, order, 1)
        into_row = lax.dot_general(
            from_col,
            direct_tile,
            (((1,), (1,)), ((), ())),
            precision=lax.Precision.HIGHEST,
            preferred_element_type=jnp.float32,
        )
        into_col = jnp.dot(
            from_row,
            mirror_tile,
            precision=lax.Precision.HIGHEST,
            preferred_element_type=jnp.float32,
        )
        total = lax.dynamic_update_slice_in_dim(
            total, lax.dynamic_slice_in_dim(total, row_start, order, 1) + into_row, row_start, 1
        )
        total = lax.dynamic_update_slice_in_dim(
            total, lax.dynamic_slice_in_dim(total, col_start, order, 1) + into_col, col_start, 1
        )
        return (total, None)

    start = jnp.zeros(field.shape, jnp.float32)
    total, _ = lax.scan(step, start, (tiles, tile_list))
    return total


def local(right_side, ridge, tiles, tile_list):
    local_width = right_side.shape[1]
    whole_rhs, whole_ridge = (
        lax.all_gather(right_side, ("grp", "tile"), axis=1, tiled=True),
        lax.all_gather(ridge, ("grp", "tile"), axis=0, tiled=True),
    )
    solution = jnp.zeros_like(whole_rhs)
    residual = whole_rhs
    direction = whole_rhs
    norm_now = gram(residual, residual)
    for step in range(ITERS):
        partial_image = apply_kernel(tiles, tile_list, direction)
        image = lax.psum(partial_image, ("grp", "tile")) + whole_ridge[None, :] * direction
        alpha = gauss_solve(gram(direction, image), norm_now)
        solution = solution + mixed(alpha, direction)
        residual = residual - mixed(alpha, image)
        if step + 1 < ITERS:
            norm_next = gram(residual, residual)
            beta = gauss_solve(norm_now, norm_next)
            direction = residual + mixed(beta, direction)
            norm_now = norm_next
    offset = lax.axis_index(("grp", "tile")) * local_width
    solution = lax.dynamic_slice_in_dim(solution, offset, local_width, 1)
    residual = lax.dynamic_slice_in_dim(residual, offset, local_width, 1)
    return (solution, residual)


def solution(mesh):
    return jax.shard_map(
        local,
        mesh=mesh,
        in_specs=(
            P(None, ("grp", "tile")),
            P(("grp", "tile")),
            P(("grp", "tile"), None, None),
            P(("grp", "tile"), None),
        ),
        out_specs=(P(None, ("grp", "tile")), P(None, ("grp", "tile"))),
        check_vma=False,
    )
```

profile of v0, /device:TPU:0, one launch (start us, length us, event | category | flops | bytes accessed | tf_op | source)
XLA Modules:
  0.0 568.1 jit_solution(14640766748409336953)
XLA Ops:
  8.0 62.1 %all-gather.2.cloned.1.call-done = f32[16,32768]{1,0:T(8,128)} async-done(((f32[16,1024]{1,0:T(8,128)}), f32[16,32768]{1,0:T(8,128)}) %all-gather.2.cloned.1.call-update) | async-done | bytes 2097168 | tf_op jit(solution)/shard_map/all_gather | solution.py:87
  72.4 57.3 %while.115 = (s32[]{:T(128)}, f32[16,32768]{1,0:T(8,128)}, s32[4,2]{0,1:T(2,128)S(1)}, f32[16,32768]{1,0:T(8,128)S(1)}, f32[4,1024,1024]{2,1,0:T(8,128)}, /*inde...) while((s32[]{:T(128)}, f32[16,32768]{1,0:T(8,128)}, s32[4,2]{0,1:T(2,128)S(1)}, ...), condition=%wide.region_1.2_spmd.clone, body=%wide.region_0.1_spmd.clone.sunk | while | flops 408977408 | bytes 8783110 | solution.py:80
  75.4 6.2 %fusion.231 = f32[16,32768]{1,0:T(8,128)} fusion(f32[16,32768]{1,0:T(8,128)} %get-tuple-element.1416, s32[]{:T(128)S(6)} %select_n.80, f32[4,1024,1024]{2,1,0:T(8,128)} %get-tuple-element.1428, s32[]{:T(128)S(6)} %copy.29, pred[]{:T(512)} %bitcast.292, f32[16,32768]{1,0:T(8,128)S(1)} %get-tuple-element.1427, s32[]{:T(128)S(6)} %select_n.81), kind=kOutput, calls=%fused_computation.21.clone.1 | convolution fusion | flops 204488704 | bytes 4391436 | tf_op jit(solution)/shard_map/while/body/eval_jaxpr/dot_general | solution.py:58
  81.7 5.1 fusion.232
  89.8 6.2 %fusion.231 = f32[16,32768]{1,0:T(8,128)} fusion(f32[16,32768]{1,0:T(8,128)} %get-tuple-element.1416, s32[]{:T(128)S(6)} %select_n.80, f32[4,1024,1024]{2,1,0:T(8,128)} %get-tuple-element.1428, s32[]{:T(128)S(6)} %copy.29, pred[]{:T(512)} %bitcast.292, f32[16,32768]{1,0:T(8,128)S(1)} %get-tuple-element.1427, s32[]{:T(128)S(6)} %select_n.81), kind=kOutput, calls=%fused_computation.21.clone.1 | convolution fusion | flops 204488704 | bytes 4391436 | tf_op jit(solution)/shard_map/while/body/eval_jaxpr/dot_general | solution.py:58
  96.0 5.1 fusion.232
  104.1 6.2 %fusion.231 = f32[16,32768]{1,0:T(8,128)} fusion(f32[16,32768]{1,0:T(8,128)} %get-tuple-element.1416, s32[]{:T(128)S(6)} %select_n.80, f32[4,1024,1024]{2,1,0:T(8,128)} %get-tuple-element.1428, s32[]{:T(128)S(6)} %copy.29, pred[]{:T(512)} %bitcast.292, f32[16,32768]{1,0:T(8,128)S(1)} %get-tuple-element.1427, s32[]{:T(128)S(6)} %select_n.81), kind=kOutput, calls=%fused_computation.21.clone.1 | convolution fusion | flops 204488704 | bytes 4391436 | tf_op jit(solution)/shard_map/while/body/eval_jaxpr/dot_general | solution.py:58
  110.3 5.1 fusion.232
  118.4 6.2 %fusion.231 = f32[16,32768]{1,0:T(8,128)} fusion(f32[16,32768]{1,0:T(8,128)} %get-tuple-element.1416, s32[]{:T(128)S(6)} %select_n.80, f32[4,1024,1024]{2,1,0:T(8,128)} %get-tuple-element.1428, s32[]{:T(128)S(6)} %copy.29, pred[]{:T(512)} %bitcast.292, f32[16,32768]{1,0:T(8,128)S(1)} %get-tuple-element.1427, s32[]{:T(128)S(6)} %select_n.81), kind=kOutput, calls=%fused_computation.21.clone.1 | convolution fusion | flops 204488704 | bytes 4391436 | tf_op jit(solution)/shard_map/while/body/eval_jaxpr/dot_general | solution.py:58
  124.7 5.1 fusion.232
  130.4 40.2 %all_gather.7 = f32[32768]{0:T(1024)S(1)} all-gather(f32[1024]{0:T(1024)S(1)} %copy-done.5), channel_id=1, replica_groups=mesh['grp'=4,'tile'=8] {'grp','tile'}, dimensions={0}, use_global_device_ids=true | all-gather | bytes 135168 | tf_op jit(solution)/shard_map/all_gather | solution.py:88
  170.6 2.9 fusion.110
  174.9 88.7 %all-reduce.3.cloned.1.call-done = f32[16,32768]{1,0:T(8,128)} async-done(((f32[16,32768]{1,0:T(8,128)}), f32[16,32768]{1,0:T(8,128)}) %all-reduce.3.cloned.1.call-update) | async-done | bytes 2097168 | tf_op jit(solution)/shard_map/psum | solution.py:96
  263.6 4.5 fusion.55
  295.6 3.6 convolution_subtract_fusion
  299.2 2.9 fusion.112
  325.3 4.3 convolution_add_fusion
  329.6 1.5 broadcast.1560
  331.2 57.8 %while.116 = (s32[]{:T(128)}, f32[16,32768]{1,0:T(8,128)}, s32[4,2]{0,1:T(2,128)S(1)}, f32[16,32768]{1,0:T(8,128)}, f32[4,1024,1024]{2,1,0:T(8,128)}, /*index=5*/s32[]{:T(128)}, s32[1,1]{0,1:T(1,128)}, s32[]{:T(128)}, s32[]{:T(128)}) while((s32[]{:T(128)}, f32[16,32768]{1,0:T(8,128)}, s32[4,2]{0,1:T(2,128)S(1)}, ...), condition=%wide.region_4.5_spmd.clone, body=%wide.region_3.4_spmd.clone.sunk | while | flops 408977408 | bytes 8783110 | solution.py:80
  334.3 6.2 %fusion.236 = f32[16,32768]{1,0:T(8,128)} fusion(f32[16,32768]{1,0:T(8,128)} %get-tuple-element.1443, s32[]{:T(128)S(6)} %select_n.84, f32[4,1024,1024]{2,1,0:T(8,128)} %get-tuple-element.1455, s32[]{:T(128)S(6)} %copy.98, pred[]{:T(512)} %bitcast.297, f32[16,32768]{1,0:T(8,128)} %get-tuple-element.1454, s32[]{:T(128)S(6)} %select_n.85), kind=kOutput, calls=%fused_computation.46.clone.1 | convolution fusion | flops 204488704 | bytes 4391436 | tf_op jit(solution)/shard_map/while/body/eval_jaxpr/dot_general | solution.py:58
  340.5 5.1 fusion.237
  348.8 6.2 %fusion.236 = f32[16,32768]{1,0:T(8,128)} fusion(f32[16,32768]{1,0:T(8,128)} %get-tuple-element.1443, s32[]{:T(128)S(6)} %select_n.84, f32[4,1024,1024]{2,1,0:T(8,128)} %get-tuple-element.1455, s32[]{:T(128)S(6)} %copy.98, pred[]{:T(512)} %bitcast.297, f32[16,32768]{1,0:T(8,128)} %get-tuple-element.1454, s32[]{:T(128)S(6)} %select_n.85), kind=kOutput, calls=%fused_computation.46.clone.1 | convolution fusion | flops 204488704 | bytes 4391436 | tf_op jit(solution)/shard_map/while/body/eval_jaxpr/dot_general | solution.py:58
  355.0 5.1 fusion.237
  363.2 6.2 %fusion.236 = f32[16,32768]{1,0:T(8,128)} fusion(f32[16,32768]{1,0:T(8,128)} %get-tuple-element.1443, s32[]{:T(128)S(6)} %select_n.84, f32[4,1024,1024]{2,1,0:T(8,128)} %get-tuple-element.1455, s32[]{:T(128)S(6)} %copy.98, pred[]{:T(512)} %bitcast.297, f32[16,32768]{1,0:T(8,128)} %get-tuple-element.1454, s32[]{:T(128)S(6)} %select_n.85), kind=kOutput, calls=%fused_computation.46.clone.1 | convolution fusion | flops 204488704 | bytes 4391436 | tf_op jit(solution)/shard_map/while/body/eval_jaxpr/dot_general | solution.py:58
  369.4 5.1 fusion.237
  377.6 6.2 %fusion.236 = f32[16,32768]{1,0:T(8,128)} fusion(f32[16,32768]{1,0:T(8,128)} %get-tuple-element.1443, s32[]{:T(128)S(6)} %select_n.84, f32[4,1024,1024]{2,1,0:T(8,128)} %get-tuple-element.1455, s32[]{:T(128)S(6)} %copy.98, pred[]{:T(512)} %bitcast.297, f32[16,32768]{1,0:T(8,128)} %get-tuple-element.1454, s32[]{:T(128)S(6)} %select_n.85), kind=kOutput, calls=%fused_computation.46.clone.1 | convolution fusion | flops 204488704 | bytes 4391436 | tf_op jit(solution)/shard_map/while/body/eval_jaxpr/dot_general | solution.py:58
  383.9 5.1 fusion.237
  389.0 3.2 fusion.111
  392.2 130.2 %all-reduce.5.cloned.1.call-done = f32[16,32768]{1,0:T(8,128)} async-done(((f32[16,32768]{1,0:T(8,128)}), f32[16,32768]{1,0:T(8,128)}) %all-reduce.5.cloned.1.call-update) | async-done | bytes 2097168 | tf_op jit(solution)/shard_map/psum | solution.py:96
  522.4 5.8 %fusion.54 = f32[16,16]{1,0:T(8,128)S(1)} fusion(f32[16,32768]{1,0:T(8,128)} %get-tuple-element.1465, f32[16,32768]{1,0:T(8,128)} %all-reduce.5.cloned.1.call-done, f32[32768]{0:T(1024)S(1)} %all_gather.7), kind=kOutput, calls=%fused_computation.60 | convolution fusion | flops 101711872 | bytes 4326400 | tf_op jit(solution)/shard_map/dot_general | solution.py:24
  554.7 1.9 fusion.113
  556.7 2.0 fusion.53
  (455 shorter events, 56.2 us)
Async XLA Ops:
  7.2 64.3 %copy-start.4 = (s32[4,2]{0,1:T(2,128)S(1)}, s32[4,2]{0,1:T(2,128)}, u32[]{:S(2)}) copy-start(s32[4,2]{0,1:T(2,128)} %param.197) | copy-start | bytes 100
  7.2 62.9 %all-gather.2.cloned.1.call-start = ((), (), s32[]{:S(2)}) async-start(), calls=%async_computation | async-start | bytes 2162688 | tf_op jit(solution)/shard_map/all_gather | solution.py:87
  7.9 255.7 %all-reduce.3.cloned.1.call-start = ((), (), s32[]{:S(2)}) async-start(), calls=%async_computation.1 | async-start | bytes 4194304 | tf_op jit(solution)/shard_map/psum | solution.py:96
  70.1 2.3 copy-start
  129.7 0.7 copy-start.5
  129.8 392.7 %all-reduce.5.cloned.1.call-start = ((), (), s32[]{:S(2)}) async-start(), calls=%async_computation.2 | async-start | bytes 4194304 | tf_op jit(solution)/shard_map/psum | solution.py:96
  299.1 2.9 copy-start.2
  522.4 32.3 %copy-start.1 = (f32[16,32768]{1,0:T(8,128)S(1)}, f32[16,32768]{1,0:T(8,128)}, u32[]{:S(2)}) copy-start(f32[16,32768]{1,0:T(8,128)} %get-tuple-element.1465) | copy-start | bytes 6291460
  554.7 1.9 copy-start.3
Sparse Core Ops, SparseCore 0:
  10.9 59.1 all-gather.1
  129.9 133.6 all-reduce.2
  389.1 133.2 all-reduce.4
where the time goes:
time: 569 us; the launch traced here: 568 us
  waiting for transfers between devices  282 us (50%)
  matrix products  122 us (21%)
  between operations  47.7 us (8%)
  local copies, waits for them, and re-layouts  40.6 us (7%)
  blocking collectives  40.2 us (7%)
  loops' own time  19.8 us (3%)
  other arithmetic  16.2 us (3%)
    psum x2, waiting for transfers between devices, local(): lax.psum(partial_image, ('grp', 'tile')) + whole_ridge[None, :] * direction  219 us
    all_gather x1, waiting for transfers between devices, local(): lax.all_gather(right_side, ('grp', 'tile'), axis=1, tiled=True)  62.1 us
    dot_general x8, matrix products, step(): lax.dot_general(from_col, direct_tile, (((1,), (1,)), ((), ())), precisio...  49.9 us
    dot_general x8, matrix products, step(): jnp.dot(from_row, mirror_tile, precision=lax.Precision.HIGHEST, preferred...  40.6 us
    all_gather x1, blocking collectives, local(): lax.all_gather(ridge, ('grp', 'tile'), axis=0, tiled=True)  40.2 us
    slice x48, local copies, waits for them, and re-layouts, gauss_solve(): scale = 1.0 / matrix[pivot, pivot]  28.1 us
    another operation x2, loops' own time, apply_kernel(): total, _ = lax.scan(step, start, (tiles, tile_list))  19.8 us
    dot_general x4, matrix products, gram(): lax.dot_general(left, right, (((1,), (1,)), ((), ())), precision=lax.Prec...  16.2 us
  transfers between devices with their start and end apart: 3, of which 3 were waited for; matrix products, arithmetic and copies ran while one was open for 1% of the time, Pallas kernels for 0%

commit v1 on v0

v1 whole, which is shorter than its diff:
```python
import functools

import jax
import jax.numpy as jnp
from jax import lax
from jax.experimental import pallas as pl
from jax.experimental.pallas import tpu as pltpu
from jax.sharding import PartitionSpec as P

ITERS = 2
MESH = pl.DeviceIdType.MESH
F32 = jnp.float32
BF16 = jnp.bfloat16
HIGH = lax.Precision.HIGHEST
NT_DIMS = (((1,), (1,)), ((), ()))


def split(x):
    hi = x.astype(BF16)
    lo = (x - hi.astype(F32)).astype(BF16)
    return jnp.concatenate([hi, lo], axis=0)


def fold(y):
    s = y.shape[0] // 2
    return y[:s] + y[s:]


def dot_nt(a, b):
    return lax.dot_general(a, b, NT_DIMS, preferred_element_type=F32)


def dot_nn(a, b):
    return jnp.dot(a, b, preferred_element_type=F32)


def gram_small(a, b):
    s = a.shape[0]
    g = dot_nt(split(a), split(b))
    g = g[:s] + g[s:]
    return g[:, :s] + g[:, s:]


def mixed(coeffs, rows):
    return jnp.dot(coeffs.T, rows, precision=HIGH, preferred_element_type=F32)


def gauss_solve(matrix, rhs):
    order = matrix.shape[0]
    aug = jnp.concatenate([matrix, rhs], axis=1)
    rows = lax.broadcasted_iota(jnp.int32, aug.shape, 0)
    for p in range(order):
        row_new = aug[p : p + 1, :] * (1.0 / aug[p : p + 1, p : p + 1])
        aug = jnp.where(rows == p, row_new, aug - aug[:, p : p + 1] * row_new)
    return aug[:, order:]


def kernel(
    grps, tiles_axis,
    list_ref, rhs_ref, ridge_ref, tiles_ref, sol_ref, res_ref,
    stage, high, low, field, image, parts, away, other0, other1, mine, came0, came1,
    small, small_sum, small_in, small_other,
    stage_sem, ag_send, ag_recv, fw_send, fw_recv, ex_send, ex_recv, rs_send, rs_recv,
    sm_send, sm_recv,
):
    half = tiles_axis // 2
    chips = grps * half
    grp = lax.axis_index("grp")
    tile = lax.axis_index("tile")
    core = lax.rem(tile, 2)
    chip = grp * half + tile // 2
    nt, order = tiles_ref.shape[0], tiles_ref.shape[1]
    s, width = rhs_ref.shape
    per = order // width

    def device(j, c):
        return (j // half, lax.rem(j, half) * 2 + c)

    partner = device(chip, 1 - core)

    def ahead(k):
        return lax.rem(chip + k, chips)

    def behind(k):
        return lax.rem(chip + chips - k, chips)

    def remote(src, dst, ssem, rsem, dev):
        return pltpu.make_async_remote_copy(
            src_ref=src, dst_ref=dst, send_sem=ssem, recv_sem=rsem, device_id=dev, device_id_type=MESH
        )

    def loads(t):
        return pltpu.make_async_copy(tiles_ref.at[t], stage.at[t], stage_sem.at[t])

    for t in range(nt):
        loads(t).start()

    barrier = pltpu.get_barrier_semaphore()
    pl.semaphore_signal(barrier, inc=1, device_id=partner, device_id_type=MESH)

    @pl.loop(1, chips)
    def _(k):
        pl.semaphore_signal(barrier, inc=1, device_id=device(ahead(k), core), device_id_type=MESH)

    pl.semaphore_wait(barrier, chips)

    def ag_copy(src, buf, it, k):
        return remote(src, buf.at[core, chip], ag_send.at[it, k], ag_recv.at[it, k], device(ahead(k), core))

    def fw_copy(src, buf, it, k):
        j = behind(k)
        return remote(src, buf.at[core, j], fw_send.at[it, k], fw_recv.at[it, k], partner)

    def gather_start(src, buf, it):
        @pl.loop(1, chips)
        def _(k):
            ag_copy(src, buf, it, k).start()

        fw_copy(src, buf, it, 0).start()

    def gather_forward(src, buf, it):
        @pl.loop(1, chips)
        def _(k):
            remote(
                src, buf.at[core, behind(k)], ag_send.at[it, k], ag_recv.at[it, k], device(ahead(k), core)
            ).wait_recv()
            fw_copy(buf.at[core, behind(k)], buf, it, k).start()

    def gather_finish(src, buf, it):
        @pl.loop(0, chips)
        def _(k):
            remote(
                src, buf.at[1 - core, behind(k)], fw_send.at[it, k], fw_recv.at[it, k], partner
            ).wait_recv()

        @pl.loop(1, chips)
        def _(k):
            ag_copy(src, buf, it, k).wait_send()
            fw_copy(buf.at[core, behind(k)], buf, it, k).wait_send()

        fw_copy(src, buf, it, 0).wait_send()

    def block(buf, b):
        pieces = []
        for i in range(per):
            p = b * per + i
            pieces.append(buf[lax.rem(p, 2), p // 2])
        return pieces[0] if per == 1 else jnp.concatenate(pieces, axis=1)

    def apply(buf, with_gram):
        total = jnp.zeros((s, s), F32)
        for t in range(nt):
            row_x = block(buf, list_ref[t, 0])
            row = split(row_x)
            col = split(block(buf, list_ref[t, 1]))
            into_row = fold(dot_nt(col, high[t]) + dot_nt(col, low[t]))
            parts[2 * t] = into_row
            parts[2 * t + 1] = fold(dot_nn(row, high[t]) + dot_nn(row, low[t]))
            if with_gram:
                g = gram_small(row_x, into_row)
                total = total + g + g.T
        return total

    def piece(p):
        b = p // per
        at = pl.ds(pl.multiple_of(lax.rem(p, per) * width, width), width)
        zero = jnp.zeros((s, width), F32)
        acc = zero
        for t in range(nt):
            acc = acc + jnp.where(list_ref[t, 0] == b, parts[2 * t, :, at], zero)
            acc = acc + jnp.where(list_ref[t, 1] == b, parts[2 * t + 1, :, at], zero)
        return acc

    def ex_copy(other, it, j):
        return remote(away.at[j], other.at[j], ex_send.at[it, j], ex_recv.at[it, j], partner)

    def rs_copy(came, it, k):
        return remote(
            mine.at[ahead(k)], came.at[k], rs_send.at[it, k], rs_recv.at[it, k], device(ahead(k), core)
        )

    def scatter_start(other, came, it):
        @pl.loop(1, chips + 1)
        def _(k):
            j = ahead(k)
            away[j] = piece(2 * j + 1 - core)
            ex_copy(other, it, j).start()

        @pl.loop(1, chips + 1)
        def _(k):
            j = ahead(k)
            mine[j] = piece(2 * j + core)

        @pl.loop(1, chips)
        def _(k):
            j = ahead(k)
            ex_copy(other, it, j).wait_recv()
            mine[j] = mine[j] + other[j]
            rs_copy(came, it, k).start()

        ex_copy(other, it, chip).wait_recv()

    def scatter_finish(other, came, it):
        def step(k, acc):
            rs_copy(came, it, k).wait_recv()
            return acc + came[k]

        total = lax.fori_loop(1, chips, step, mine[chip] + other[chip])

        @pl.loop(1, chips)
        def _(k):
            rs_copy(came, it, k).wait_send()

        @pl.loop(0, chips)
        def _(j):
            ex_copy(other, it, j).wait_send()

        return total

    def gram_all(first, second):
        def step(j, acc):
            for c in range(2):
                acc = acc + gram_small(first[c, j], second[c, j])
            return acc

        return lax.fori_loop(0, chips, step, jnp.zeros((s, s), F32), unroll=4)

    gather_start(rhs_ref, field, 0)
    field[core, chip] = rhs_ref[...]

    chunk = min(128, order)
    for t in range(nt):
        loads(t).wait()
        differ = list_ref[t, 0] != list_ref[t, 1]

        @pl.loop(0, order // chunk)
        def _(i):
            at = pl.ds(pl.multiple_of(i * chunk, chunk), chunk)
            x = stage[t, at, :]
            rows = lax.broadcasted_iota(jnp.int32, x.shape, 0) + i * chunk
            cols = lax.broadcasted_iota(jnp.int32, x.shape, 1)
            weight = jnp.where(rows > cols, 1.0, jnp.where(rows == cols, 0.5, 0.0))
            weight = jnp.where(differ, 1.0, weight)
            x = x * weight
            hi = x.astype(BF16)
            high[t, at, :] = hi
            low[t, at, :] = (x - hi.astype(F32)).astype(BF16)

    gather_forward(rhs_ref, field, 0)
    gather_finish(rhs_ref, field, 0)

    apply(field, False)
    scatter_start(other0, came0, 0)
    norm0 = gram_all(field, field)
    own_rhs = rhs_ref[...]
    own_ridge = ridge_ref[...]
    own_image = scatter_finish(other0, came0, 0) + own_ridge * own_rhs
    image[core, chip] = own_image
    gather_start(image.at[core, chip], image, 1)
    gather_forward(image.at[core, chip], image, 1)
    gather_finish(image.at[core, chip], image, 1)

    alpha = gauss_solve(gram_all(field, image), norm0)

    def residual_step(j, acc):
        for c in range(2):
            r = field[c, j] - mixed(alpha, image[c, j])
            image[c, j] = r
            acc = acc + gram_small(r, r)
        return acc

    norm1 = lax.fori_loop(0, chips, residual_step, jnp.zeros((s, s), F32), unroll=2)
    beta = gauss_solve(norm0, norm1)

    @pl.loop(0, chips, unroll=2)
    def _(j):
        for c in range(2):
            field[c, j] = image[c, j] + mixed(beta, field[c, j])

    partial = apply(field, True)
    own_dir = field[core, chip]
    partial = partial + gram_small(own_dir, own_dir * own_ridge)
    pad = jnp.concatenate([partial, jnp.zeros((s, 128 - s), F32)], axis=1)
    small[...] = pad
    sm_ex = remote(small, small_other, sm_send.at[0], sm_recv.at[0], partner)
    sm_ex.start()
    scatter_start(other1, came1, 1)
    sm_ex.wait_recv()
    small_sum[...] = pad + small_other[...]

    def sm_copy(k):
        return remote(small_sum, small_in.at[k], sm_send.at[k], sm_recv.at[k], device(ahead(k), core))

    @pl.loop(1, chips)
    def _(k):
        sm_copy(k).start()

    sol_ref[...] = mixed(alpha, own_rhs)

    def sm_step(k, acc):
        sm_copy(k).wait_recv()
        return acc + small_in[k]

    pq = lax.fori_loop(1, chips, sm_step, small_sum[...])[:, :s]
    alpha1 = gauss_solve(pq, norm1)
    sol_ref[...] = sol_ref[...] + mixed(alpha1, own_dir)
    last = scatter_finish(other1, came1, 1) + own_ridge * own_dir
    res_ref[...] = image[core, chip] - mixed(alpha1, last)

    @pl.loop(1, chips)
    def _(k):
        sm_copy(k).wait_send()

    sm_ex.wait_send()


def solution(mesh):
    grps, tiles_axis = mesh.shape["grp"], mesh.shape["tile"]
    chips = grps * tiles_axis // 2

    def local(right_side, ridge, tiles, tile_list):
        s, width = right_side.shape
        nt, order = tiles.shape[0], tiles.shape[1]
        vmem = pl.BlockSpec(memory_space=pltpu.VMEM)
        out = jax.ShapeDtypeStruct((s, width), F32)
        dma = pltpu.SemaphoreType.DMA
        return pl.pallas_call(
            functools.partial(kernel, grps, tiles_axis),
            out_shape=(out, out),
            in_specs=[
                pl.BlockSpec(memory_space=pltpu.SMEM),
                vmem,
                vmem,
                pl.BlockSpec(memory_space=pl.ANY),
            ],
            out_specs=(vmem, vmem),
            scratch_shapes=[
                pltpu.VMEM((nt, order, order), F32),
                pltpu.VMEM((nt, order, order), BF16),
                pltpu.VMEM((nt, order, order), BF16),
                pltpu.VMEM((2, chips, s, width), F32),
                pltpu.VMEM((2, chips, s, width), F32),
                pltpu.VMEM((2 * nt, s, order), F32),
                pltpu.VMEM((chips, s, width), F32),
                pltpu.VMEM((chips, s, width), F32),
                pltpu.VMEM((chips, s, width), F32),
                pltpu.VMEM((chips, s, width), F32),
                pltpu.VMEM((chips, s, width), F32),
                pltpu.VMEM((chips, s, width), F32),
                pltpu.VMEM((s, 128), F32),
                pltpu.VMEM((s, 128), F32),
                pltpu.VMEM((chips, s, 128), F32),
                pltpu.VMEM((s, 128), F32),
                dma((nt,)),
                dma((2, chips)),
                dma((2, chips)),
                dma((2, chips)),
                dma((2, chips)),
                dma((2, chips)),
                dma((2, chips)),
                dma((2, chips)),
                dma((2, chips)),
                dma((chips,)),
                dma((chips,)),
            ],
            compiler_params=pltpu.CompilerParams(
                collective_id=0, has_side_effects=True, vmem_limit_bytes=60 * 1024 * 1024
            ),
        )(tile_list, right_side, ridge[None, :], tiles)

    return jax.shard_map(
        local,
        mesh=mesh,
        in_specs=(
            P(None, ("grp", "tile")),
            P(("grp", "tile")),
            P(("grp", "tile"), None, None),
            P(("grp", "tile"), None),
        ),
        out_specs=(P(None, ("grp", "tile")), P(None, ("grp", "tile"))),
        check_vma=False,
    )
```

time: 569 us -> 160 us (0.28)
  waiting for transfers between devices: 282 us -> 0 us
  Pallas kernels: 0 us -> 155 us
  matrix products: 122 us -> 0 us
  between operations: 47.7 us -> 0.64 us
  blocking collectives: 40.2 us -> 0 us
  local copies, waits for them, and re-layouts: 40.6 us -> 4.28 us
  loops' own time: 19.8 us -> 0 us
  other arithmetic: 16.2 us -> 0 us
    psum x2 -> x0, waiting for transfers between devices: 219 us -> none  [local(): lax.psum(partial_image, ('grp', 'tile')) + whole_ridge[None, :] * direction]
    pallas_call x0 -> x1, Pallas kernels: none -> 155 us  [local(): pl.pallas_call(functools.partial(kernel, grps, tiles_axis), out_shape=(ou...]
    dot_general x25 -> x0, matrix products: 122 us -> none  [the longest x8 49.9 us: step(): lax.dot_general(from_col, direct_tile, (((1,), (1,)), ((), ())), precisio...]
    all_gather x1 -> x0, waiting for transfers between devices: 62.1 us -> none  [local(): lax.all_gather(right_side, ('grp', 'tile'), axis=1, tiled=True)]
    all_gather x1 -> x0, blocking collectives: 40.2 us -> none  [local(): lax.all_gather(ridge, ('grp', 'tile'), axis=0, tiled=True)]
    slice x56 -> x0, local copies, waits for them, and re-layouts: 32.3 us -> none  [the longest x48 28.1 us: gauss_solve(): scale = 1.0 / matrix[pivot, pivot]]
    another operation x2 -> x0, loops' own time: 19.8 us -> none  [apply_kernel(): total, _ = lax.scan(step, start, (tiles, tile_list))]
    mul x229 -> x0, other arithmetic: 9.64 us -> none  [the longest x48 8.54 us: gauss_solve(): matrix[:, pivot] * (1.0 - (jnp.arange(order) == pivot).astype(matrix.dtype))]
  transfers between devices with their start and end apart: 3 -> 0, of which waited for: 3 -> 0; matrix products, arithmetic and copies ran while one was open for 1% -> 0% of each run, Pallas kernels for 0% -> 0%
where the time goes in v1:
time: 160 us
  Pallas kernels  155 us (97%)
  local copies, waits for them, and re-layouts  4.28 us (3%)
    pallas_call x1, Pallas kernels, local(): pl.pallas_call(functools.partial(kernel, grps, tiles_axis), out_shape=(ou...  155 us
    unnamed x3, local copies, waits for them, and re-layouts  4.28 us

profile of v1, /device:TPU:0, one launch (start us, length us, event | category | flops | bytes accessed | tf_op | source)
XLA Modules:
  0.0 159.7 jit_solution(11765411284712348609)
XLA Ops:
  0.6 1.3 copy.6.list_ref
  2.0 154.8 %shard_map.59 = (f32[16,1024]{1,0:T(8,128)}, f32[16,1024]{1,0:T(8,128)}) custom-call(s32[4,2]{1,0:T(4,128)} %copy.6.list_ref, f32[16,1024]{1,0:T(8,128)} %rhs_ref.1, f32[1,1024]{1,0:T(1,128)} %bitcast.1, f32[4,1024,1024]{2,1,0:T(8,128)} %tiles_ref.1), custom_call_target="tpu_custom_call" | custom-call | tf_op jit(solution)/shard_map/pallas_call | solution.py:327
  156.8 1.5 copy.9
  158.2 1.5 copy.10

commit v2 on v1

--- a/solution.py
+++ b/solution.py
@@ -60,15 +60,16 @@
     list_ref, rhs_ref, ridge_ref, tiles_ref, sol_ref, res_ref,
     stage, high, low, field, image, parts, away, other0, other1, mine, came0, came1,
     small, small_sum, small_in, small_other,
-    stage_sem, ag_send, ag_recv, fw_send, fw_recv, ex_send, ex_recv, rs_send, rs_recv,
-    sm_send, sm_recv,
+    stage_sem, agz_send, agz_recv, agq_send, agq_recv, fw_send, fw_recv, ex_send, ex_recv,
+    rsz_send, rsz_recv, rsq_send, rsq_recv, sm_send, sm_recv, smq_send, smq_recv, smz_send, smz_recv,
 ):
     half = tiles_axis // 2
     chips = grps * half
     grp = lax.axis_index("grp")
     tile = lax.axis_index("tile")
     core = lax.rem(tile, 2)
-    chip = grp * half + tile // 2
+    place = tile // 2
+    chip = grp * half + place
     nt, order = tiles_ref.shape[0], tiles_ref.shape[1]
     s, width = rhs_ref.shape
     per = order // width
@@ -78,11 +79,11 @@
 
     partner = device(chip, 1 - core)
 
-    def ahead(k):
-        return lax.rem(chip + k, chips)
-
-    def behind(k):
-        return lax.rem(chip + chips - k, chips)
+    def ahead(kz, kq):
+        return lax.rem(grp + kz, grps) * half + lax.rem(place + kq, half)
+
+    def behind(kz, kq):
+        return lax.rem(grp + grps - kz, grps) * half + lax.rem(place + half - kq, half)
 
     def remote(src, dst, ssem, rsem, dev):
         return pltpu.make_async_remote_copy(
@@ -98,47 +99,62 @@
     barrier = pltpu.get_barrier_semaphore()
     pl.semaphore_signal(barrier, inc=1, device_id=partner, device_id_type=MESH)
 
-    @pl.loop(1, chips)
-    def _(k):
-        pl.semaphore_signal(barrier, inc=1, device_id=device(ahead(k), core), device_id_type=MESH)
-
-    pl.semaphore_wait(barrier, chips)
-
-    def ag_copy(src, buf, it, k):
-        return remote(src, buf.at[core, chip], ag_send.at[it, k], ag_recv.at[it, k], device(ahead(k), core))
-
-    def fw_copy(src, buf, it, k):
-        j = behind(k)
-        return remote(src, buf.at[core, j], fw_send.at[it, k], fw_recv.at[it, k], partner)
+    for kz in range(1, grps):
+        pl.semaphore_signal(barrier, inc=1, device_id=device(ahead(kz, 0), core), device_id_type=MESH)
+    for kq in range(1, half):
+        pl.semaphore_signal(barrier, inc=1, device_id=device(ahead(0, kq), core), device_id_type=MESH)
+    pl.semaphore_wait(barrier, grps + half - 1)
+
+    def ag_z(src, buf, it, kz):
+        return remote(src, buf.at[core, chip], agz_send.at[it, kz], agz_recv.at[it, kz], device(ahead(kz, 0), core))
+
+    def ag_q(src, buf, it, kz, kq):
+        return remote(
+            src, buf.at[core, behind(kz, 0)], agq_send.at[it, kz, kq], agq_recv.at[it, kz, kq], device(ahead(0, kq), core)
+        )
+
+    def fw_copy(src, buf, it, kz, kq):
+        return remote(src, buf.at[core, behind(kz, kq)], fw_send.at[it, kz, kq], fw_recv.at[it, kz, kq], partner)
+
+    def spread(src, buf, it, kz):
+        for kq in range(1, half):
+            ag_q(src, buf, it, kz, kq).start()
+        fw_copy(src, buf, it, kz, 0).start()
 
     def gather_start(src, buf, it):
-        @pl.loop(1, chips)
-        def _(k):
-            ag_copy(src, buf, it, k).start()
-
-        fw_copy(src, buf, it, 0).start()
-
-    def gather_forward(src, buf, it):
-        @pl.loop(1, chips)
-        def _(k):
-            remote(
-                src, buf.at[core, behind(k)], ag_send.at[it, k], ag_recv.at[it, k], device(ahead(k), core)
-            ).wait_recv()
-            fw_copy(buf.at[core, behind(k)], buf, it, k).start()
+        for kz in range(1, grps):
+            ag_z(src, buf, it, kz).start()
+        spread(src, buf, it, 0)
+
+    def gather_spread(buf, it, kz):
+        mine_now = buf.at[core, behind(kz, 0)]
+        remote(
+            mine_now, mine_now, agz_send.at[it, kz], agz_recv.at[it, kz], device(ahead(kz, 0), core)
+        ).wait_recv()
+        spread(mine_now, buf, it, kz)
+
+    def gather_forward(buf, it):
+        for kz in range(grps):
+            for kq in range(1, half):
+                mine_now = buf.at[core, behind(kz, kq)]
+                remote(
+                    mine_now, mine_now, agq_send.at[it, kz, kq], agq_recv.at[it, kz, kq], device(ahead(0, kq), core)
+                ).wait_recv()
+                fw_copy(mine_now, buf, it, kz, kq).start()
 
     def gather_finish(src, buf, it):
-        @pl.loop(0, chips)
-        def _(k):
-            remote(
-                src, buf.at[1 - core, behind(k)], fw_send.at[it, k], fw_recv.at[it, k], partner
-            ).wait_recv()
-
-        @pl.loop(1, chips)
-        def _(k):
-            ag_copy(src, buf, it, k).wait_send()
-            fw_copy(buf.at[core, behind(k)], buf, it, k).wait_send()
-
-        fw_copy(src, buf, it, 0).wait_send()
+        for kz in range(grps):
+            for kq in range(half):
+                other_now = buf.at[1 - core, behind(kz, kq)]
+                remote(other_now, other_now, fw_send.at[it, kz, kq], fw_recv.at[it, kz, kq], partner).wait_recv()
+        for kz in range(grps):
+            held = src if kz == 0 else buf.at[core, behind(kz, 0)]
+            if kz > 0:
+                ag_z(src, buf, it, kz).wait_send()
+            for kq in range(half):
+                if kq > 0:
+                    ag_q(held, buf, it, kz, kq).wait_send()
+                fw_copy(held if kq == 0 else buf.at[core, behind(kz, kq)], buf, it, kz, kq).wait_send()
 
     def block(buf, b):
         pieces = []
@@ -174,47 +190,67 @@
     def ex_copy(other, it, j):
         return remote(away.at[j], other.at[j], ex_send.at[it, j], ex_recv.at[it, j], partner)
 
-    def rs_copy(came, it, k):
+    def rsq_copy(came, it, kz, kq):
         return remote(
-            mine.at[ahead(k)], came.at[k], rs_send.at[it, k], rs_recv.at[it, k], device(ahead(k), core)
-        )
+            mine.at[ahead(kz, kq)], came.at[kz, kq], rsq_send.at[it, kz, kq], rsq_recv.at[it, kz, kq],
+            device(ahead(0, kq), core),
+        )
+
+    def rsz_copy(came, it, kz):
+        return remote(
+            mine.at[ahead(kz, 0)], came.at[kz, 0], rsz_send.at[it, kz], rsz_recv.at[it, kz],
+            device(ahead(kz, 0), core),
+        )
+
+    zs = list(range(1, grps)) + [0]
+    qs = list(range(1, half)) + [0]
 
     def scatter_start(other, came, it):
-        @pl.loop(1, chips + 1)
-        def _(k):
-            j = ahead(k)
+        def order_of(i):
+            return ahead(lax.rem(i // half + 1, grps), lax.rem(lax.rem(i, half) + 1, half))
+
+        @pl.loop(0, chips)
+        def _(i):
+            j = order_of(i)
             away[j] = piece(2 * j + 1 - core)
             ex_copy(other, it, j).start()
 
-        @pl.loop(1, chips + 1)
-        def _(k):
-            j = ahead(k)
+        @pl.loop(0, chips)
+        def _(i):
+            j = order_of(i)
             mine[j] = piece(2 * j + core)
 
-        @pl.loop(1, chips)
-        def _(k):
-            j = ahead(k)
-            ex_copy(other, it, j).wait_recv()
-            mine[j] = mine[j] + other[j]
-            rs_copy(came, it, k).start()
-
-        ex_copy(other, it, chip).wait_recv()
-
-    def scatter_finish(other, came, it):
-        def step(k, acc):
-            rs_copy(came, it, k).wait_recv()
-            return acc + came[k]
-
-        total = lax.fori_loop(1, chips, step, mine[chip] + other[chip])
-
-        @pl.loop(1, chips)
-        def _(k):
-            rs_copy(came, it, k).wait_send()
-
-        @pl.loop(0, chips)
-        def _(j):
-            ex_copy(other, it, j).wait_send()
-
+        for kz in zs:
+            for kq in qs:
+                j = ahead(kz, kq)
+                ex_copy(other, it, j).wait_recv()
+                mine[j] = mine[j] + other[j]
+                if kq > 0:
+                    rsq_copy(came, it, kz, kq).start()
+
+    def scatter_columns(came, it):
+        for kz in zs:
+            j = ahead(kz, 0)
+            acc = mine[j]
+            for kq in range(1, half):
+                rsq_copy(came, it, kz, kq).wait_recv()
+                acc = acc + came[kz, kq]
+            mine[j] = acc
+            if kz > 0:
+                rsz_copy(came, it, kz).start()
+
+    def scatter_finish(came, it):
+        total = mine[chip]
+        for kz in range(1, grps):
+            rsz_copy(came, it, kz).wait_recv()
+            total = total + came[kz, 0]
+        for kz in range(grps):
+            if kz > 0:
+                rsz_copy(came, it, kz).wait_send()
+            for kq in range(half):
+                if kq > 0:
+                    rsq_copy(came, it, kz, kq).wait_send()
+                ex_copy(other0, it, ahead(kz, kq)).wait_send()
         return total
 
     def gram_all(first, second):
@@ -229,7 +265,8 @@
     field[core, chip] = rhs_ref[...]
 
     chunk = min(128, order)
-    for t in range(nt):
+
+    def prepare(t):
         loads(t).wait()
         differ = list_ref[t, 0] != list_ref[t, 1]
 
@@ -246,18 +283,26 @@
             high[t, at, :] = hi
             low[t, at, :] = (x - hi.astype(F32)).astype(BF16)
 
-    gather_forward(rhs_ref, field, 0)
+    for i in range(max(nt, grps - 1)):
+        if i < nt:
+            prepare(i)
+        if i + 1 < grps:
+            gather_spread(field, 0, i + 1)
+    gather_forward(field, 0)
     gather_finish(rhs_ref, field, 0)
 
     apply(field, False)
     scatter_start(other0, came0, 0)
+    scatter_columns(came0, 0)
     norm0 = gram_all(field, field)
     own_rhs = rhs_ref[...]
     own_ridge = ridge_ref[...]
-    own_image = scatter_finish(other0, came0, 0) + own_ridge * own_rhs
+    own_image = scatter_finish(came0, 0) + own_ridge * own_rhs
     image[core, chip] = own_image
     gather_start(image.at[core, chip], image, 1)
-    gather_forward(image.at[core, chip], image, 1)
+    for kz in range(1, grps):
+        gather_spread(image, 1, kz)
+    gather_forward(image, 1)
     gather_finish(image.at[core, chip], image, 1)
 
     alpha = gauss_solve(gram_all(field, image), norm0)
@@ -286,37 +331,49 @@
     sm_ex.start()
     scatter_start(other1, came1, 1)
     sm_ex.wait_recv()
-    small_sum[...] = pad + small_other[...]
-
-    def sm_copy(k):
-        return remote(small_sum, small_in.at[k], sm_send.at[k], sm_recv.at[k], device(ahead(k), core))
-
-    @pl.loop(1, chips)
-    def _(k):
-        sm_copy(k).start()
-
+    small_sum[0] = pad + small_other[...]
+
+    def smq_copy(kq):
+        return remote(
+            small_sum.at[0], small_in.at[0, kq], smq_send.at[kq], smq_recv.at[kq], device(ahead(0, kq), core)
+        )
+
+    def smz_copy(kz):
+        return remote(
+            small_sum.at[1], small_in.at[1, kz], smz_send.at[kz], smz_recv.at[kz], device(ahead(kz, 0), core)
+        )
+
+    for kq in range(1, half):
+        smq_copy(kq).start()
+    acc = small_sum[0]
+    for kq in range(1, half):
+        smq_copy(kq).wait_recv()
+        acc = acc + small_in[0, kq]
+    small_sum[1] = acc
+    for kz in range(1, grps):
+        smz_copy(kz).start()
+    scatter_columns(came1, 1)
     sol_ref[...] = mixed(alpha, own_rhs)
-
-    def sm_step(k, acc):
-        sm_copy(k).wait_recv()
-        return acc + small_in[k]
-
-    pq = lax.fori_loop(1, chips, sm_step, small_sum[...])[:, :s]
+    for kz in range(1, grps):
+        smz_copy(kz).wait_recv()
+        acc = acc + small_in[1, kz]
+    pq = acc[:, :s]
     alpha1 = gauss_solve(pq, norm1)
     sol_ref[...] = sol_ref[...] + mixed(alpha1, own_dir)
-    last = scatter_finish(other1, came1, 1) + own_ridge * own_dir
+    last = scatter_finish(came1, 1) + own_ridge * own_dir
     res_ref[...] = image[core, chip] - mixed(alpha1, last)
 
-    @pl.loop(1, chips)
-    def _(k):
-        sm_copy(k).wait_send()
-
+    for kq in range(1, half):
+        smq_copy(kq).wait_send()
+    for kz in range(1, grps):
+        smz_copy(kz).wait_send()
     sm_ex.wait_send()
 
 
 def solution(mesh):
     grps, tiles_axis = mesh.shape["grp"], mesh.shape["tile"]
-    chips = grps * tiles_axis // 2
+    half = tiles_axis // 2
+    chips = grps * half
 
     def local(right_side, ridge, tiles, tile_list):
         s, width = right_side.shape
@@ -345,23 +402,31 @@
                 pltpu.VMEM((chips, s, width), F32),
                 pltpu.VMEM((chips, s, width), F32),
                 pltpu.VMEM((chips, s, width), F32),
-                pltpu.VMEM((chips, s, width), F32),
-                pltpu.VMEM((chips, s, width), F32),
+                pltpu.VMEM((grps, half, s, width), F32),
+                pltpu.VMEM((grps, half, s, width), F32),
                 pltpu.VMEM((s, 128), F32),
-                pltpu.VMEM((s, 128), F32),
-                pltpu.VMEM((chips, s, 128), F32),
+                pltpu.VMEM((2, s, 128), F32),
+                pltpu.VMEM((2, max(half, grps), s, 128), F32),
                 pltpu.VMEM((s, 128), F32),
                 dma((nt,)),
+                dma((2, grps)),
+                dma((2, grps)),
+                dma((2, grps, half)),
+                dma((2, grps, half)),
+                dma((2, grps, half)),
+                dma((2, grps, half)),
                 dma((2, chips)),
                 dma((2, chips)),
-                dma((2, chips)),
-                dma((2, chips)),
-                dma((2, chips)),
-                dma((2, chips)),
-                dma((2, chips)),
-                dma((2, chips)),
-                dma((chips,)),
-                dma((chips,)),
+                dma((2, grps)),
+                dma((2, grps)),
+                dma((2, grps, half)),
+                dma((2, grps, half)),
+                dma((1,)),
+                dma((1,)),
+                dma((half,)),
+                dma((half,)),
+                dma((grps,)),
+                dma((grps,)),
             ],
             compiler_params=pltpu.CompilerParams(
                 collective_id=0, has_side_effects=True, vmem_limit_bytes=60 * 1024 * 1024

time: 160 us -> 118 us (0.74)
  Pallas kernels: 155 us -> 112 us
    pallas_call x1, Pallas kernels: 155 us -> 112 us  [local(): pl.pallas_call(functools.partial(kernel, grps, tiles_axis), out_shape=(ou...]
where the time goes in v2:
time: 118 us; the launch traced here: 117 us
  Pallas kernels  112 us (95%)
  local copies, waits for them, and re-layouts  4.28 us (4%)
    pallas_call x1, Pallas kernels, local(): pl.pallas_call(functools.partial(kernel, grps, tiles_axis), out_shape=(ou...  112 us
    unnamed x3, local copies, waits for them, and re-layouts  4.28 us

profile of v2, /device:TPU:0, one launch (start us, length us, event | category | flops | bytes accessed | tf_op | source)
XLA Modules:
  0.0 117.4 jit_solution(4550686732400482562)
XLA Ops:
  0.6 1.3 %copy.6.list_ref = s32[4,2]{1,0:T(4,128)} copy(s32[4,2]{0,1:T(2,128)} %param.7) | data formatting | bytes 64 | tf_op args[3]
  2.0 112.5 %shard_map.59 = (f32[16,1024]{1,0:T(8,128)}, f32[16,1024]{1,0:T(8,128)}) custom-call(s32[4,2]{1,0:T(4,128)} %copy.6.list_ref, f32[16,1024]{1,0:T(8,128)} %rhs_ref.1, f32[1,1024]{1,0:T(1,128)} %bitcast.1, f32[4,1024,1024]{2,1,0:T(8,128)} %tiles_ref.1), custom_call_target="tpu_custom_call" | custom-call | tf_op jit(solution)/shard_map/pallas_call | solution.py:384
  114.4 1.5 %copy.9 = f32[16,1024]{1,0:T(8,128)} copy(f32[16,1024]{1,0:T(8,128)} %get-tuple-element.4) | data formatting | bytes 131072
  115.9 1.5 %copy.10 = f32[16,1024]{1,0:T(8,128)} copy(f32[16,1024]{1,0:T(8,128)} %get-tuple-element.5) | data formatting | bytes 131072

commit v3 on v2

--- a/solution.py
+++ b/solution.py
@@ -41,8 +41,8 @@
     return g[:, :s] + g[:, s:]
 
 
-def mixed(coeffs, rows):
-    return jnp.dot(coeffs.T, rows, precision=HIGH, preferred_element_type=F32)
+def mixed(coeffs_t, rows):
+    return jnp.dot(coeffs_t, rows, precision=HIGH, preferred_element_type=F32)
 
 
 def gauss_solve(matrix, rhs):
@@ -58,7 +58,7 @@
 def kernel(
     grps, tiles_axis,
     list_ref, rhs_ref, ridge_ref, tiles_ref, sol_ref, res_ref,
-    stage, high, low, field, image, parts, away, other0, other1, mine, came0, came1,
+    stage, high, low, field, image, parts0, parts1, away, other0, other1, mine, came0, came1,
     small, small_sum, small_in, small_other,
     stage_sem, agz_send, agz_recv, agq_send, agq_recv, fw_send, fw_recv, ex_send, ex_recv,
     rsz_send, rsz_recv, rsq_send, rsq_recv, sm_send, sm_recv, smq_send, smq_recv, smz_send, smz_recv,
@@ -133,20 +133,25 @@
         ).wait_recv()
         spread(mine_now, buf, it, kz)
 
-    def gather_forward(buf, it):
+    def gather_forward(buf, it, meet, acc):
         for kz in range(grps):
             for kq in range(1, half):
-                mine_now = buf.at[core, behind(kz, kq)]
+                j = behind(kz, kq)
+                mine_now = buf.at[core, j]
                 remote(
                     mine_now, mine_now, agq_send.at[it, kz, kq], agq_recv.at[it, kz, kq], device(ahead(0, kq), core)
                 ).wait_recv()
                 fw_copy(mine_now, buf, it, kz, kq).start()
-
-    def gather_finish(src, buf, it):
+                acc = meet(acc, core, j)
+        return acc
+
+    def gather_finish(src, buf, it, meet, acc):
         for kz in range(grps):
             for kq in range(half):
-                other_now = buf.at[1 - core, behind(kz, kq)]
+                j = behind(kz, kq)
+                other_now = buf.at[1 - core, j]
                 remote(other_now, other_now, fw_send.at[it, kz, kq], fw_recv.at[it, kz, kq], partner).wait_recv()
+                acc = meet(acc, 1 - core, j)
         for kz in range(grps):
             held = src if kz == 0 else buf.at[core, behind(kz, 0)]
             if kz > 0:
@@ -155,6 +160,7 @@
                 if kq > 0:
                     ag_q(held, buf, it, kz, kq).wait_send()
                 fw_copy(held if kq == 0 else buf.at[core, behind(kz, kq)], buf, it, kz, kq).wait_send()
+        return acc
 
     def block(buf, b):
         pieces = []
@@ -163,21 +169,14 @@
             pieces.append(buf[lax.rem(p, 2), p // 2])
         return pieces[0] if per == 1 else jnp.concatenate(pieces, axis=1)
 
-    def apply(buf, with_gram):
-        total = jnp.zeros((s, s), F32)
+    def apply(buf, parts):
         for t in range(nt):
-            row_x = block(buf, list_ref[t, 0])
-            row = split(row_x)
+            row = split(block(buf, list_ref[t, 0]))
             col = split(block(buf, list_ref[t, 1]))
-            into_row = fold(dot_nt(col, high[t]) + dot_nt(col, low[t]))
-            parts[2 * t] = into_row
+            parts[2 * t] = fold(dot_nt(col, high[t]) + dot_nt(col, low[t]))
             parts[2 * t + 1] = fold(dot_nn(row, high[t]) + dot_nn(row, low[t]))
-            if with_gram:
-                g = gram_small(row_x, into_row)
-                total = total + g + g.T
-        return total
-
-    def piece(p):
+
+    def piece(p, parts):
         b = p // per
         at = pl.ds(pl.multiple_of(lax.rem(p, per) * width, width), width)
         zero = jnp.zeros((s, width), F32)
@@ -205,20 +204,20 @@
     zs = list(range(1, grps)) + [0]
     qs = list(range(1, half)) + [0]
 
-    def scatter_start(other, came, it):
+    def scatter_start(other, came, it, parts):
         def order_of(i):
             return ahead(lax.rem(i // half + 1, grps), lax.rem(lax.rem(i, half) + 1, half))
 
         @pl.loop(0, chips)
         def _(i):
             j = order_of(i)
-            away[j] = piece(2 * j + 1 - core)
+            away[j] = piece(2 * j + 1 - core, parts)
             ex_copy(other, it, j).start()
 
         @pl.loop(0, chips)
         def _(i):
             j = order_of(i)
-            mine[j] = piece(2 * j + core)
+            mine[j] = piece(2 * j + core, parts)
 
         for kz in zs:
             for kq in qs:
@@ -288,48 +287,62 @@
             prepare(i)
         if i + 1 < grps:
             gather_spread(field, 0, i + 1)
-    gather_forward(field, 0)
-    gather_finish(rhs_ref, field, 0)
-
-    apply(field, False)
-    scatter_start(other0, came0, 0)
+    def nothing(acc, c, j):
+        return acc
+
+    gather_forward(field, 0, nothing, None)
+    gather_finish(rhs_ref, field, 0, nothing, None)
+
+    apply(field, parts0)
+    scatter_start(other0, came0, 0, parts0)
+    norm0 = gram_all(field, field)
     scatter_columns(came0, 0)
-    norm0 = gram_all(field, field)
     own_rhs = rhs_ref[...]
     own_ridge = ridge_ref[...]
     own_image = scatter_finish(came0, 0) + own_ridge * own_rhs
     image[core, chip] = own_image
     gather_start(image.at[core, chip], image, 1)
+
+    def meet(acc, c, j):
+        return acc + gram_small(field[c, j], image[c, j])
+
+    pq = gram_small(own_rhs, own_image)
     for kz in range(1, grps):
         gather_spread(image, 1, kz)
-    gather_forward(image, 1)
-    gather_finish(image.at[core, chip], image, 1)
-
-    alpha = gauss_solve(gram_all(field, image), norm0)
+        pq = meet(pq, core, behind(kz, 0))
+    pq = gather_forward(image, 1, meet, pq)
+    pq = gather_finish(image.at[core, chip], image, 1, meet, pq)
+
+    apply(image, parts1)
+    scatter_start(other1, came1, 1, parts1)
+    alpha = gauss_solve(pq, norm0)
+    alpha_t = alpha.T
 
     def residual_step(j, acc):
         for c in range(2):
-            r = field[c, j] - mixed(alpha, image[c, j])
-            image[c, j] = r
+            r = field[c, j] - mixed(alpha_t, image[c, j])
             acc = acc + gram_small(r, r)
         return acc
 
     norm1 = lax.fori_loop(0, chips, residual_step, jnp.zeros((s, s), F32), unroll=2)
     beta = gauss_solve(norm0, norm1)
-
-    @pl.loop(0, chips, unroll=2)
-    def _(j):
-        for c in range(2):
-            field[c, j] = image[c, j] + mixed(beta, field[c, j])
-
-    partial = apply(field, True)
-    own_dir = field[core, chip]
-    partial = partial + gram_small(own_dir, own_dir * own_ridge)
+    beta_t = beta.T
+
+    def onward(first, second):
+        return (first - mixed(alpha_t, second)) + mixed(beta_t, first)
+
+    own_res = own_rhs - mixed(alpha_t, own_image)
+    own_dir = own_res + mixed(beta_t, own_rhs)
+    partial = gram_small(own_dir, own_dir * own_ridge)
+    for t in range(nt):
+        b = list_ref[t, 0]
+        g = gram_small(onward(block(field, b), block(image, b)), onward(parts0[2 * t], parts1[2 * t]))
+        partial = partial + g + g.T
     pad = jnp.concatenate([partial, jnp.zeros((s, 128 - s), F32)], axis=1)
     small[...] = pad
     sm_ex = remote(small, small_other, sm_send.at[0], sm_recv.at[0], partner)
     sm_ex.start()
-    scatter_start(other1, came1, 1)
+    scatter_columns(came1, 1)
     sm_ex.wait_recv()
     small_sum[0] = pad + small_other[...]
 
@@ -352,16 +365,14 @@
     small_sum[1] = acc
     for kz in range(1, grps):
         smz_copy(kz).start()
-    scatter_columns(came1, 1)
-    sol_ref[...] = mixed(alpha, own_rhs)
+    sol_ref[...] = mixed(alpha_t, own_rhs)
     for kz in range(1, grps):
         smz_copy(kz).wait_recv()
         acc = acc + small_in[1, kz]
-    pq = acc[:, :s]
-    alpha1 = gauss_solve(pq, norm1)
-    sol_ref[...] = sol_ref[...] + mixed(alpha1, own_dir)
-    last = scatter_finish(came1, 1) + own_ridge * own_dir
-    res_ref[...] = image[core, chip] - mixed(alpha1, last)
+    alpha1_t = gauss_solve(acc[:, :s], norm1).T
+    sol_ref[...] = sol_ref[...] + mixed(alpha1_t, own_dir)
+    spread_image = scatter_finish(came1, 1) + own_ridge * own_image
+    res_ref[...] = own_res - mixed(alpha1_t, onward(own_image, spread_image))
 
     for kq in range(1, half):
         smq_copy(kq).wait_send()
@@ -398,6 +409,7 @@
                 pltpu.VMEM((2, chips, s, width), F32),
                 pltpu.VMEM((2, chips, s, width), F32),
                 pltpu.VMEM((2 * nt, s, order), F32),
+                pltpu.VMEM((2 * nt, s, order), F32),
                 pltpu.VMEM((chips, s, width), F32),
                 pltpu.VMEM((chips, s, width), F32),
                 pltpu.VMEM((chips, s, width), F32),

time: 118 us -> 105 us (0.89)
  Pallas kernels: 112 us -> 100 us
    pallas_call x1, Pallas kernels: 112 us -> 100 us  [local(): pl.pallas_call(functools.partial(kernel, grps, tiles_axis), out_shape=(ou...]
where the time goes in v3:
time: 105 us
  Pallas kernels  100 us (95%)
  local copies, waits for them, and re-layouts  4.28 us (4%)
    pallas_call x1, Pallas kernels, local(): pl.pallas_call(functools.partial(kernel, grps, tiles_axis), out_shape=(ou...  100 us
    unnamed x3, local copies, waits for them, and re-layouts  4.28 us

profile of v3, /device:TPU:0, one launch (start us, length us, event | category | flops | bytes accessed | tf_op | source)
XLA Modules:
  0.0 104.9 jit_solution(10747067892002989598)
XLA Ops:
  0.6 1.3 %copy.6.list_ref = s32[4,2]{1,0:T(4,128)} copy(s32[4,2]{0,1:T(2,128)} %param.7) | data formatting | bytes 64 | tf_op args[3]
  2.0 100.0 %shard_map.59 = (f32[16,1024]{1,0:T(8,128)}, f32[16,1024]{1,0:T(8,128)}) custom-call(s32[4,2]{1,0:T(4,128)} %copy.6.list_ref, f32[16,1024]{1,0:T(8,128)} %rhs_ref.1, f32[1,1024]{1,0:T(1,128)} %bitcast.1, f32[4,1024,1024]{2,1,0:T(8,128)} %tiles_ref.1), custom_call_target="tpu_custom_call" | custom-call | tf_op jit(solution)/shard_map/pallas_call | solution.py:395
  101.9 1.5 %copy.9 = f32[16,1024]{1,0:T(8,128)} copy(f32[16,1024]{1,0:T(8,128)} %get-tuple-element.4) | data formatting | bytes 131072
  103.4 1.5 %copy.10 = f32[16,1024]{1,0:T(8,128)} copy(f32[16,1024]{1,0:T(8,128)} %get-tuple-element.5) | data formatting | bytes 131072

commit v4 on v3

--- a/solution.py
+++ b/solution.py
@@ -41,8 +41,20 @@
     return g[:, :s] + g[:, s:]
 
 
-def mixed(coeffs_t, rows):
-    return jnp.dot(coeffs_t, rows, precision=HIGH, preferred_element_type=F32)
+def terms(x):
+    h = x.astype(BF16).astype(F32)
+    m = (x - h).astype(BF16).astype(F32)
+    return h, m, x - h - m
+
+
+def mixer(coeffs_t):
+    h, m, l = terms(coeffs_t)
+    return jnp.concatenate([h, h, m, m, h, l], axis=1).astype(BF16)
+
+
+def mixed(coeffs, rows):
+    h, m, l = (x.astype(BF16) for x in terms(rows))
+    return dot_nn(coeffs, jnp.concatenate([h, m, h, m, l, h], axis=0))
 
 
 def gauss_solve(matrix, rhs):
@@ -316,7 +328,7 @@
     apply(image, parts1)
     scatter_start(other1, came1, 1, parts1)
     alpha = gauss_solve(pq, norm0)
-    alpha_t = alpha.T
+    alpha_t = mixer(alpha.T)
 
     def residual_step(j, acc):
         for c in range(2):
@@ -324,9 +336,9 @@
             acc = acc + gram_small(r, r)
         return acc
 
-    norm1 = lax.fori_loop(0, chips, residual_step, jnp.zeros((s, s), F32), unroll=2)
+    norm1 = lax.fori_loop(0, chips, residual_step, jnp.zeros((s, s), F32), unroll=4)
     beta = gauss_solve(norm0, norm1)
-    beta_t = beta.T
+    beta_t = mixer(beta.T)
 
     def onward(first, second):
         return (first - mixed(alpha_t, second)) + mixed(beta_t, first)
@@ -369,7 +381,7 @@
     for kz in range(1, grps):
         smz_copy(kz).wait_recv()
         acc = acc + small_in[1, kz]
-    alpha1_t = gauss_solve(acc[:, :s], norm1).T
+    alpha1_t = mixer(gauss_solve(acc[:, :s], norm1).T)
     sol_ref[...] = sol_ref[...] + mixed(alpha1_t, own_dir)
     spread_image = scatter_finish(came1, 1) + own_ridge * own_image
     res_ref[...] = own_res - mixed(alpha1_t, onward(own_image, spread_image))

time: 105 us -> 102 us (0.971)
  Pallas kernels: 100 us -> 96.9 us
    pallas_call x1, Pallas kernels: 100 us -> 96.9 us  [local(): pl.pallas_call(functools.partial(kernel, grps, tiles_axis), out_shape=(ou...]
where the time goes in v4:
time: 102 us
  Pallas kernels  96.9 us (95%)
  local copies, waits for them, and re-layouts  4.28 us (4%)
    pallas_call x1, Pallas kernels, local(): pl.pallas_call(functools.partial(kernel, grps, tiles_axis), out_shape=(ou...  96.9 us
    unnamed x3, local copies, waits for them, and re-layouts  4.28 us

profile of v4, /device:TPU:0, one launch (start us, length us, event | category | flops | bytes accessed | tf_op | source)
XLA Modules:
  0.0 101.8 jit_solution(15359630909472616006)
XLA Ops:
  0.6 1.3 %copy.6.list_ref = s32[4,2]{1,0:T(4,128)} copy(s32[4,2]{0,1:T(2,128)} %param.7) | data formatting | bytes 64 | tf_op args[3]
  2.0 96.9 %shard_map.59 = (f32[16,1024]{1,0:T(8,128)}, f32[16,1024]{1,0:T(8,128)}) custom-call(s32[4,2]{1,0:T(4,128)} %copy.6.list_ref, f32[16,1024]{1,0:T(8,128)} %rhs_ref.1, f32[1,1024]{1,0:T(1,128)} %bitcast.1, f32[4,1024,1024]{2,1,0:T(8,128)} %tiles_ref.1), custom_call_target="tpu_custom_call" | custom-call | tf_op jit(solution)/shard_map/pallas_call | solution.py:407
  98.9 1.5 %copy.9 = f32[16,1024]{1,0:T(8,128)} copy(f32[16,1024]{1,0:T(8,128)} %get-tuple-element.4) | data formatting | bytes 131072
  100.3 1.5 %copy.10 = f32[16,1024]{1,0:T(8,128)} copy(f32[16,1024]{1,0:T(8,128)} %get-tuple-element.5) | data formatting | bytes 131072
